TPU v7x, 128 devices: a whole 4x4x4 slice. The times are simulated.
128 devices in a mesh: row: 16 (over z, y), col: 8 (over x, core).
Axes of the slice: x: 4, y: 4, z: 4, core: 2. Of those that a mesh axis runs over, the one named last changes fastest.
Arguments:
- covariance: bfloat16 [28672, 28672], P('row', 'col'), may hold values from -1 to 8, as said below
- right_side: float32 [28672, 256], P(('col', 'row')), may hold values from -50 to 50
Outputs:
- solution: float32 [28672, 256], P(('col', 'row'))
- residual: float32 [28672, 256], P(('col', 'row'))
- direction: float32 [28672, 256], P(('col', 'row'))
Inputs may be any that keep to these rules, and one draw needn't show every extreme that they name: `covariance`: symmetric and positive definite, with condition number under 100.
All inputs are finite; a program needn't handle non-finite values.
Results may differ from a plain program's by a relative error of at most 0.0158.
Values may be sent and summed in bfloat16 or wider, within the bound.
A program may use at most 128 MiB of HBM per device.

v0:
```python
import jax
import jax.numpy as jnp
from jax import lax
from jax.sharding import PartitionSpec as P

ITERS = 3


HIGHEST_PRECISION = lax.Precision.HIGHEST


def broadcast(block, axis, owner):
    block = jnp.where(lax.axis_index(axis) == owner, block, jnp.zeros_like(block))
    return lax.psum(block, axis)


def inner_product(left_block, right_block):
    return lax.dot_general(
        left_block,
        right_block,
        (((0,), (0,)), ((), ())),
        precision=HIGHEST_PRECISION,
        preferred_element_type=jnp.float32,
    )


def apply_small(block, coeffs):
    return jnp.dot(block, coeffs, precision=HIGHEST_PRECISION, preferred_element_type=jnp.float32)


def symmetric_part(matrix):
    return 0.5 * (matrix + matrix.T)


def solve_spd(matrix, rhs_block):
    factor = jnp.linalg.cholesky(matrix)
    return jax.scipy.linalg.cho_solve((factor, True), rhs_block)


def gram_total(pieces):
    return lax.psum((pieces[0],), ("row", "col"))


def row_block(column_rows):
    fold_ratio = lax.axis_size("row") // lax.axis_size("col")
    row_index = lax.axis_index("row")
    block_rows = column_rows.shape[0] // fold_ratio
    selected = lax.dynamic_slice_in_dim(
        column_rows, row_index % fold_ratio * block_rows, block_rows, 0
    )
    return broadcast(selected, "col", row_index // fold_ratio)


def body(covariance, right_side):
    residual = right_side
    solution = jnp.zeros_like(residual)
    direction = residual
    norm_now = gram_total((inner_product(residual, residual),))[0]
    for iteration in range(ITERS):
        lowered = direction.astype(jnp.bfloat16)
        column_rows = lax.all_gather(lowered, "row", axis=0, tiled=True)
        own_rows = row_block(column_rows)
        image = lax.psum_scatter(
            lax.dot_general(
                covariance, own_rows, (((0,), (0,)), ((), ())), preferred_element_type=jnp.float32
            ),
            "row",
            scatter_dimension=0,
            tiled=True,
        )
        curvature = symmetric_part(gram_total((inner_product(direction, image),))[0])
        alpha = solve_spd(curvature, norm_now)
        solution = solution + apply_small(direction, alpha)
        residual = residual - apply_small(image, alpha)
        norm_next = gram_total((inner_product(residual, residual),))[0]
        beta = solve_spd(norm_now, norm_next)
        direction = residual + apply_small(direction, beta)
        norm_now = norm_next
    return (solution, residual, direction)


def solution(mesh):
    return jax.shard_map(
        body,
        mesh=mesh,
        in_specs=(P("row", "col"), P(("col", "row"), None)),
        out_specs=(P(("col", "row"), None), P(("col", "row"), None), P(("col", "row"), None)),
        check_vma=False,
    )
```

profile of v0, /device:TPU:1, one launch (start us, length us, event | category | flops | bytes accessed | tf_op | source)
XLA Modules:
  0.0 1700.8 jit_solution(4524802082663702419)
XLA Ops:
  8.9 48.2 %all-gather.4.cloned.1.call-done = bf16[3584,256]{1,0:T(8,128)(2,1)} async-done(((bf16[224,256]{1,0:T(8,128)(2,1)}), bf16[3584,256]{1,0:T(8,128)(2,1)}) %all-gather.4.cloned.1.call-update) | async-done | bytes 1835024 | tf_op jit(solution)/shard_map/all_gather | solution.py:61
  59.4 60.8 %all-reduce.12.cloned.1.call-done = bf16[1792,256]{1,0:T(8,128)(2,1)} async-done(((bf16[1792,256]{1,0:T(8,128)(2,1)}), bf16[1792,256]{1,0:T(8,128)(2,1)}) %all-reduce.12.cloned.1.call-update) | async-done | bytes 917520 | tf_op jit(solution)/shard_map/psum | solution.py:14
  120.3 10.3 convolution_bitcast_fusion.2
  130.6 5.1 copy.35
  138.0 75.0 %reduce-scatter.10.cloned.1.call-done = f32[224,256]{1,0:T(8,128)} async-done(((f32[3584,256]{1,0:T(8,128)}), f32[224,256]{1,0:T(8,128)}) %reduce-scatter.10.cloned.1.call-update) | async-done | bytes 229392
  215.9 149.5 %all-reduce.28.cloned.1.call-done = (f32[256,256]{0,1:T(8,128)}, f32[256,256]{1,0:T(8,128)}) async-done(((f32[256,256]{0,1:T(8,128)}, f32[256,256]{1,0:T(8,128)}), (f32[256,256]{0,1:T(8,128)}, f32[256,256]{1,0:T(8,128)})) %all-reduce.28.cloned.1.call-update) | async-done | bytes 524304 | tf_op jit(solution)/shard_map/psum | solution.py:41
  367.7 11.7 cholesky.298
  379.5 9.8 custom-call.23
  389.8 11.7 cholesky.315
  407.8 19.7 %custom-call.24 = f32[2,128,128]{1,2,0:T(8,128)S(1)} custom-call(f32[2,128,128]{2,1,0:T(8,128)S(1)} %get-tuple-element.43), custom_call_target="InvertDiagBlocksLowerTriangular" | custom-call | tf_op jit(solution)/shard_map/jit(_cho_solve)/triangular_solve | solution.py:37
  431.3 11.7 cholesky.332
  443.1 9.8 custom-call.25
  453.4 11.7 cholesky.349
  467.1 4.2 while.13
  471.4 19.7 %custom-call.26 = f32[2,128,128]{1,2,0:T(8,128)S(1)} custom-call(f32[2,128,128]{2,1,0:T(8,128)S(1)} %get-tuple-element.44), custom_call_target="InvertDiagBlocksLowerTriangular" | custom-call | tf_op jit(solution)/shard_map/jit(_cho_solve)/triangular_solve | solution.py:37
  491.1 82.8 %all-reduce.14.cloned.1.call-done = f32[256,256]{0,1:T(8,128)} async-done(((f32[256,256]{0,1:T(8,128)}), f32[256,256]{0,1:T(8,128)}) %all-reduce.14.cloned.1.call-update) | async-done | bytes 262160 | tf_op jit(solution)/shard_map/psum | solution.py:41
  578.6 40.7 %all-gather.6.cloned.1.call-done = bf16[3584,256]{1,0:T(8,128)(2,1)} async-done(((bf16[224,256]{1,0:T(8,128)(2,1)}), bf16[3584,256]{1,0:T(8,128)(2,1)}) %all-gather.6.cloned.1.call-update) | async-done | bytes 1835024 | tf_op jit(solution)/shard_map/all_gather | solution.py:61
  621.6 60.8 %all-reduce.16.cloned.1.call-done = bf16[1792,256]{1,0:T(8,128)(2,1)} async-done(((bf16[1792,256]{1,0:T(8,128)(2,1)}), bf16[1792,256]{1,0:T(8,128)(2,1)}) %all-reduce.16.cloned.1.call-update) | async-done | bytes 917520 | tf_op jit(solution)/shard_map/psum | solution.py:14
  682.5 10.3 convolution_bitcast_fusion.1
  692.8 5.1 copy.37
  699.0 11.7 cholesky.400
  710.8 9.8 custom-call.29
  721.1 11.7 cholesky.417
  735.5 40.0 %reduce-scatter.12.cloned.1.call-done = f32[224,256]{1,0:T(8,128)} async-done(((f32[3584,256]{1,0:T(8,128)}), f32[224,256]{1,0:T(8,128)}) %reduce-scatter.12.cloned.1.call-update) | async-done | bytes 229392
  778.0 146.2 %all-reduce.18.cloned.1.call-done = f32[256,256]{1,0:T(8,128)} async-done(((f32[256,256]{1,0:T(8,128)}), f32[256,256]{1,0:T(8,128)}) %all-reduce.18.cloned.1.call-update) | async-done | bytes 262160 | tf_op jit(solution)/shard_map/psum | solution.py:41
  926.5 11.7 cholesky.366
  938.3 9.8 custom-call.27
  948.6 11.7 cholesky.383
  963.1 4.3 while.14
  967.5 19.7 %custom-call.28 = f32[2,128,128]{1,2,0:T(8,128)S(1)} custom-call(f32[2,128,128]{2,1,0:T(8,128)S(1)} %get-tuple-element.45), custom_call_target="InvertDiagBlocksLowerTriangular" | custom-call | tf_op jit(solution)/shard_map/jit(_cho_solve)/triangular_solve | solution.py:37
  994.8 19.7 %custom-call.30 = f32[2,128,128]{1,2,0:T(8,128)S(1)} custom-call(f32[2,128,128]{2,1,0:T(8,128)S(1)} %get-tuple-element.46), custom_call_target="InvertDiagBlocksLowerTriangular" | custom-call | tf_op jit(solution)/shard_map/jit(_cho_solve)/triangular_solve | solution.py:37
  1014.5 117.2 %all-reduce.20.cloned.1.call-done = f32[256,256]{0,1:T(8,128)} async-done(((f32[256,256]{0,1:T(8,128)}), f32[256,256]{0,1:T(8,128)}) %all-reduce.20.cloned.1.call-update) | async-done | bytes 262160 | tf_op jit(solution)/shard_map/psum | solution.py:41
  1136.5 40.7 %all-gather.8.cloned.1.call-done = bf16[3584,256]{1,0:T(8,128)(2,1)} async-done(((bf16[224,256]{1,0:T(8,128)(2,1)}), bf16[3584,256]{1,0:T(8,128)(2,1)}) %all-gather.8.cloned.1.call-update) | async-done | bytes 1835024 | tf_op jit(solution)/shard_map/all_gather | solution.py:61
  1179.5 60.8 %all-reduce.22.cloned.1.call-done = bf16[1792,256]{1,0:T(8,128)(2,1)} async-done(((bf16[1792,256]{1,0:T(8,128)(2,1)}), bf16[1792,256]{1,0:T(8,128)(2,1)}) %all-reduce.22.cloned.1.call-update) | async-done | bytes 917520 | tf_op jit(solution)/shard_map/psum | solution.py:14
  1240.3 10.3 convolution_bitcast_fusion
  1250.7 5.6 copy.39
  1257.4 11.7 cholesky.468
  1269.2 9.8 custom-call.33
  1279.4 11.7 cholesky.485
  1293.8 39.9 %reduce-scatter.14.cloned.1.call-done = f32[224,256]{1,0:T(8,128)} async-done(((f32[3584,256]{1,0:T(8,128)}), f32[224,256]{1,0:T(8,128)}) %reduce-scatter.14.cloned.1.call-update) | async-done | bytes 229392
  1336.1 4.3 while.17
  1340.3 19.7 %custom-call.34 = f32[2,128,128]{1,2,0:T(8,128)S(1)} custom-call(f32[2,128,128]{2,1,0:T(8,128)S(1)} %get-tuple-element.48), custom_call_target="InvertDiagBlocksLowerTriangular" | custom-call | tf_op jit(solution)/shard_map/jit(_cho_solve)/triangular_solve | solution.py:37
  1360.0 122.4 %all-reduce.24.cloned.1.call-done = f32[256,256]{1,0:T(8,128)} async-done(((f32[256,256]{1,0:T(8,128)}), f32[256,256]{1,0:T(8,128)}) %all-reduce.24.cloned.1.call-update) | async-done | bytes 262160 | tf_op jit(solution)/shard_map/psum | solution.py:41
  1484.8 11.7 cholesky.434
  1496.6 9.8 custom-call.31
  1506.9 11.7 cholesky.451
  1525.3 19.9 %custom-call.32 = f32[2,128,128]{1,2,0:T(8,128)S(1)} custom-call(f32[2,128,128]{2,1,0:T(8,128)S(1)} %get-tuple-element.47), custom_call_target="InvertDiagBlocksLowerTriangular" | custom-call | tf_op jit(solution)/shard_map/jit(_cho_solve)/triangular_solve | solution.py:37
  1549.8 139.6 %all-reduce.26.cloned.1.call-done = f32[256,256]{1,0:T(8,128)} async-done(((f32[256,256]{1,0:T(8,128)}), f32[256,256]{1,0:T(8,128)}) %all-reduce.26.cloned.1.call-update) | async-done | bytes 262160 | tf_op jit(solution)/shard_map/psum | solution.py:41
  (219 shorter events, 100.0 us)
Async XLA Ops:
  7.2 49.9 %all-gather.4.cloned.1.call-start = ((), (), s32[]{:S(2)}) async-start(), calls=%async_computation.3 | async-start | bytes 1949696 | tf_op jit(solution)/shard_map/all_gather | solution.py:61
  8.8 111.4 %all-reduce.12.cloned.1.call-start = ((), (), s32[]{:S(2)}) async-start(), calls=%async_computation.4 | async-start | bytes 1835008 | tf_op jit(solution)/shard_map/psum | solution.py:14
  59.4 153.6 %reduce-scatter.10.cloned.1.call-start = ((), (), s32[]{:S(2)}) async-start(), calls=%async_computation.14 | async-start | bytes 3899392
  135.7 0.9 copy-start
  135.7 229.6 %all-reduce.28.cloned.1.call-start = ((), (), s32[]{:S(2)}) async-start(), calls=%async_computation.17 | async-start | bytes 1048576 | tf_op jit(solution)/shard_map/psum | solution.py:41
  215.3 358.5 %all-reduce.14.cloned.1.call-start = ((), (), s32[]{:S(2)}) async-start(), calls=%async_computation.5 | async-start | bytes 524288 | tf_op jit(solution)/shard_map/psum | solution.py:41
  365.3 62.1 %copy-start.4 = (f32[256,256]{0,1:T(8,128)S(1)}, f32[256,256]{0,1:T(8,128)}, u32[]{:S(2)}) copy-start(f32[256,256]{0,1:T(8,128)} %get-tuple-element.97) | copy-start | bytes 786436
  366.5 63.0 %copy-start.7 = (f32[224,256]{1,0:T(8,128)S(1)}, f32[224,256]{1,0:T(8,128)}, u32[]{:S(2)}) copy-start(f32[224,256]{1,0:T(8,128)} %reduce-scatter.10.cloned.1.call-done) | copy-start | bytes 688132
  431.2 188.1 %all-gather.6.cloned.1.call-start = ((), (), s32[]{:S(2)}) async-start(), calls=%async_computation.6 | async-start | bytes 1949696 | tf_op jit(solution)/shard_map/all_gather | solution.py:61
  578.6 103.9 %all-reduce.16.cloned.1.call-start = ((), (), s32[]{:S(2)}) async-start(), calls=%async_computation.7 | async-start | bytes 1835008 | tf_op jit(solution)/shard_map/psum | solution.py:14
  621.6 153.9 %reduce-scatter.12.cloned.1.call-start = ((), (), s32[]{:S(2)}) async-start(), calls=%async_computation.15 | async-start | bytes 3899392
  697.9 0.9 copy-start.2
  697.9 226.3 %all-reduce.18.cloned.1.call-start = ((), (), s32[]{:S(2)}) async-start(), calls=%async_computation.8 | async-start | bytes 524288 | tf_op jit(solution)/shard_map/psum | solution.py:41
  777.8 353.9 %all-reduce.20.cloned.1.call-start = ((), (), s32[]{:S(2)}) async-start(), calls=%async_computation.9 | async-start | bytes 524288 | tf_op jit(solution)/shard_map/psum | solution.py:41
  925.3 63.7 %copy-start.6 = (f32[224,256]{1,0:T(8,128)S(1)}, f32[224,256]{1,0:T(8,128)}, u32[]{:S(2)}) copy-start(f32[224,256]{1,0:T(8,128)} %reduce-scatter.12.cloned.1.call-done) | copy-start | bytes 688132
  990.8 186.4 %all-gather.8.cloned.1.call-start = ((), (), s32[]{:S(2)}) async-start(), calls=%async_computation.10 | async-start | bytes 1949696 | tf_op jit(solution)/shard_map/all_gather | solution.py:61
  1136.4 103.9 %all-reduce.22.cloned.1.call-start = ((), (), s32[]{:S(2)}) async-start(), calls=%async_computation.11 | async-start | bytes 1835008 | tf_op jit(solution)/shard_map/psum | solution.py:14
  1179.5 154.2 %reduce-scatter.14.cloned.1.call-start = ((), (), s32[]{:S(2)}) async-start(), calls=%async_computation.16 | async-start | bytes 3899392
  1256.2 0.9 copy-start.1
  1256.3 226.2 %all-reduce.24.cloned.1.call-start = ((), (), s32[]{:S(2)}) async-start(), calls=%async_computation.12 | async-start | bytes 524288 | tf_op jit(solution)/shard_map/psum | solution.py:41
  1336.0 353.5 %all-reduce.26.cloned.1.call-start = ((), (), s32[]{:S(2)}) async-start(), calls=%async_computation.13 | async-start | bytes 524288 | tf_op jit(solution)/shard_map/psum | solution.py:41
  1483.6 63.5 %copy-start.5 = (f32[224,256]{1,0:T(8,128)S(1)}, f32[224,256]{1,0:T(8,128)}, u32[]{:S(2)}) copy-start(f32[224,256]{1,0:T(8,128)} %reduce-scatter.14.cloned.1.call-done) | copy-start | bytes 688132
  1547.4 146.6 %copy-start.3 = (f32[224,256]{1,0:T(8,128)}, f32[224,256]{1,0:T(8,128)S(1)}, u32[]{:S(2)}) copy-start(f32[224,256]{1,0:T(8,128)S(1)} %convolution_subtract_fusion) | copy-start | bytes 688132
Sparse Core Ops, SparseCore 0:
  10.7 46.3 all-gather.3
  59.5 60.7 all-reduce.11
  135.8 77.1 reduce-scatter.9
  217.8 147.5 all-reduce.27
  431.3 142.4 all-reduce.13
  578.7 40.5 all-gather.5
  621.7 60.7 all-reduce.15
  698.0 77.4 reduce-scatter.11
  780.3 143.8 all-reduce.17
  990.9 140.7 all-reduce.19
  1136.6 40.5 all-gather.7
  1179.6 60.7 all-reduce.21
  1256.4 77.2 reduce-scatter.13
  1338.3 144.0 all-reduce.23
  1548.9 140.5 all-reduce.25
where the time goes:
time: 1710 us; the launch traced here: 1700 us
  waiting for transfers between devices  1220 us (71%)
  other arithmetic  337 us (20%)
  matrix products  68.1 us (4%)
  local copies, waits for them, and re-layouts  45.5 us (3%)
  between operations  22.9 us (1%)
    psum x6, waiting for transfers between devices, gram_total(): return lax.psum((pieces[0],), ('row', 'col'))  758 us
    another operation x40, other arithmetic, solve_spd(): factor = jnp.linalg.cholesky(matrix)  206 us
    psum x3, waiting for transfers between devices, broadcast(): return lax.psum(block, axis)  182 us
    unnamed x18, waiting for transfers between devices  155 us
    all_gather x3, waiting for transfers between devices, body(): column_rows = lax.all_gather(lowered, 'row', axis=0, tiled=True)  130 us
    another operation x13, other arithmetic, solve_spd(): return jax.scipy.linalg.cho_solve((factor, True), rhs_block)  118 us
  transfers between devices with their start and end apart: 15, of which 15 were waited for; matrix products, arithmetic and copies ran while one was open for 11% of the time, Pallas kernels for 0%

commit v1 on v0

v1 whole, which is shorter than its diff:
```python
import functools

import jax
import jax.numpy as jnp
from jax import lax
from jax.experimental import pallas as pl
from jax.experimental.pallas import tpu as pltpu
from jax.sharding import PartitionSpec as P

ITERS = 3
MESH = pl.DeviceIdType.MESH
HIGHEST = lax.Precision.HIGHEST
F32 = jnp.float32
BF16 = jnp.bfloat16
WIRE = jnp.bfloat16
SIDE = 256
HALF = SIDE // 2
RING = 4
OFFS = (0, -1, 1, 2)


def mm(left, right):
    return jnp.dot(left, right, precision=HIGHEST, preferred_element_type=F32)


def mm_t(left, right):
    return lax.dot_general(
        left, right, (((0,), (0,)), ((), ())), precision=HIGHEST, preferred_element_type=F32
    )


def gauss_jordan(mats, size):
    row = lax.broadcasted_iota(jnp.int32, (size, 1), 0)
    lane = lax.broadcasted_iota(jnp.int32, (1, size), 1)
    mats = list(mats)
    for k in range(size):
        for i, m in enumerate(mats):
            inv = 1.0 / m[k : k + 1, k : k + 1]
            pivot_row = jnp.where(lane == k, 1.0, m[k : k + 1, :]) * inv
            pivot_col = jnp.where(row == k, -1.0, m[:, k : k + 1])
            rest = jnp.where((row == k) | (lane == k), 0.0, m)
            mats[i] = rest - pivot_col * pivot_row
    return mats


def kernel(
    a_hbm, b_ref, x_ref, r_ref, d_ref,
    a, lb, part, s1, t1, s2, t2, s3, t3, rp, dp, qp, q,
    g, gt, g0, u1, g1, u2, g2, u3, h1, h0, gf, norm, full, inv, work, tri, small,
    a_sem, ag_send, ag_recv, rs_send, rs_recv, pm_send, pm_recv, ar_send, ar_recv,
):
    row, col = lax.axis_index("row"), lax.axis_index("col")
    z, y, x, core = row // RING, row % RING, col // 2, col % 2
    here = (x, y, z)

    def wrap(v):
        return (v + 2 * RING) % RING

    def device(pos, c):
        return (pos[2] * RING + pos[1], pos[0] * 2 + c)

    def along(axis, d):
        pos = list(here)
        pos[axis] = wrap(pos[axis] + d)
        return device(pos, core)

    other_core = device(here, 1 - core)

    def remote(src, dst, send, recv, target):
        return pltpu.make_async_remote_copy(
            src_ref=src, dst_ref=dst, send_sem=send, recv_sem=recv, device_id=target, device_id_type=MESH
        )

    load_a = pltpu.make_async_copy(a_hbm, a, a_sem)
    load_a.start()

    piece_out = col * 16 + row
    to_rows = (piece_out // 8, piece_out % 8)
    piece_in = row * 8 + col
    to_owner = (piece_in % 16, piece_in // 16)
    fixed = piece_out == piece_in

    barrier = pltpu.get_barrier_semaphore()

    def greet(target):
        pl.semaphore_signal(barrier, inc=1, device_id=target, device_id_type=MESH)

    for axis in range(3):
        for d in range(1, RING):
            greet(along(axis, d))
    greet(other_core)

    @pl.when(jnp.logical_not(fixed))
    def _():
        greet(to_rows)
        greet(to_owner)

    pl.semaphore_wait(barrier, jnp.where(fixed, 10, 12))

    def permute(src, dst, target, n):
        copy = remote(src, dst, pm_send.at[n], pm_recv.at[n], target)

        @pl.when(jnp.logical_not(fixed))
        def _():
            copy.start()

        @pl.when(fixed)
        def _():
            pltpu.make_async_copy(src, dst, pm_recv.at[n]).start()

        return copy

    def permute_wait(copy):
        copy.wait_recv()

        @pl.when(jnp.logical_not(fixed))
        def _():
            copy.wait_send()

    rows_in = permute(b_ref, rp, to_rows, 0)

    r_ref[...] = b_ref[...]
    d_ref[...] = b_ref[...]
    x_ref[...] = jnp.zeros_like(x_ref)

    def region(h, c1, c2, rows):
        zc, yc = (c2, c1) if h == 0 else (c1, c2)
        return lb.at[zc, yc, h, rows]

    def gather(h, g_, e, incoming):
        axes = (1, 2) if h == 0 else (2, 1)
        mine = (here[axes[0]], here[axes[1]])
        if incoming:
            off = (-1, 1, 2, 2)[e]
        else:
            off = (0, 0, -1, 1)[e]
        rows = (pl.ds(0, 112), pl.ds(0, 112), pl.ds(0, 64), pl.ds(64, 48))[e]
        if g_ == 0:
            c1, c2, axis = wrap(mine[0] + off), mine[1], axes[0]
        else:
            c1, c2, axis = wrap(mine[0] + OFFS[g_ - 1]), wrap(mine[1] + off), axes[1]
        ref = region(h, c1, c2, rows)
        n = h * 20 + g_ * 4 + e
        return remote(ref, ref, ag_send.at[n], ag_recv.at[n], along(axis, 1 if e % 2 == 0 else -1))

    def send(h, g_, *es):
        for e in es:
            gather(h, g_, e, False).start()

    def take(h, g_, *es):
        for e in es:
            gather(h, g_, e, True).wait_recv()

    def product(zc, j, first):
        cols = pl.ds(pl.multiple_of(zc * 896, 128), 896)
        block = lb[zc].reshape(896, SIDE)
        out = jnp.dot(a[j, :, cols], block, preferred_element_type=F32)
        if first:
            part[j] = out
        else:
            part[j] += out

    def all_products(zc, first):
        def body(j, carry):
            product(zc, j, first)
            return carry

        lax.fori_loop(0, 8, body, 0)

    def core_copy(i):
        return remote(s1.at[i], t1.at[i], rs_send.at[i], rs_recv.at[i], other_core)

    def ring_copy(src, dst, n, d):
        return remote(src, dst, rs_send.at[n], rs_recv.at[n], along(0, d))

    def reduce_copy(stage, m, d, src, dst):
        axis = (m + stage) % 3
        n = 2 + (stage * 3 + m) * 3 + d - 1
        return remote(src, dst, ar_send.at[n], ar_recv.at[n], along(axis, d))

    def spread_copy(stage, m, d, src, dst):
        axis = (m + stage) % 3
        n = 29 + (stage * 3 + m) * 3 + d - 1
        return remote(src, dst, ar_send.at[n], ar_recv.at[n], along(axis, d))

    def iteration(it, carry):
        lb[z, y] = d_ref[...].astype(BF16).reshape(2, 112, SIDE)
        for h in (0, 1):
            send(h, 0, 0, 1)
            send(h, 1, 0, 1)

        @pl.when(it > 0)
        def _():
            rp[...] = rp[...] - mm(qp[...], small[0])
            dp[...] = rp[...] + mm(dp[...], small[1])

        for h in (0, 1):
            take(h, 0, 0)
            send(h, 0, 2)
            send(h, 2, 0, 1)
        for h in (0, 1):
            take(h, 0, 1)
            send(h, 0, 3)
            send(h, 3, 0, 1)
        for h in (0, 1):
            take(h, 1, 0)
            send(h, 1, 2)
            take(h, 1, 1)
            send(h, 1, 3)
        for h in (0, 1):
            take(h, 0, 2, 3)
            send(h, 4, 0, 1)

        @pl.when(it == 0)
        def _():
            load_a.wait()

        for h in (0, 1):
            take(h, 2, 0)
            send(h, 2, 2)
            take(h, 2, 1)
            send(h, 2, 3)
        take(1, 1, 2, 3)
        all_products(z, True)
        for h in (0, 1):
            take(h, 3, 0)
            send(h, 3, 2)
            take(h, 3, 1)
            send(h, 3, 3)
        for h in (0, 1):
            take(h, 4, 0)
            send(h, 4, 2)
            take(h, 4, 1)
            send(h, 4, 3)
        take(1, 2, 2, 3)
        all_products(wrap(z - 1), False)
        take(1, 3, 2, 3)
        all_products(wrap(z + 1), False)
        take(1, 4, 2, 3)
        for g_ in (1, 2, 3, 4):
            take(0, g_, 2, 3)

        last = wrap(z + 2)

        def finish(i, c_):
            off = jnp.where(i == 0, 2, jnp.where(i == 1, 1, jnp.where(i == 2, 3, 0)))
            xc = (x + off) % RING
            j = 2 * xc + 1 - core
            product(last, j, False)
            s1[i] = part[j].astype(WIRE)
            core_copy(i).start()
            product(last, 2 * xc + core, False)
            return c_

        lax.fori_loop(0, 4, finish, 0)

        def chip_sum(i, off):
            core_copy(i).wait_recv()
            return part[2 * wrap(x + off) + core] + t1[i].astype(F32)

        far = chip_sum(0, 2)
        s2[0] = far[:112].astype(WIRE)
        s2[1] = far[112:].astype(WIRE)
        step = [
            ring_copy(s2.at[0], t2.at[0], 4, 1),
            ring_copy(s2.at[1], t2.at[1], 5, -1),
            ring_copy(s3.at[0], t3.at[0], 6, 1),
            ring_copy(s3.at[1], t3.at[1], 7, -1),
        ]
        step[0].start()
        step[1].start()
        right = chip_sum(1, 1)
        s3[0, 112:] = right[112:].astype(WIRE)
        step[0].wait_recv()
        s3[0, :112] = (right[:112] + t2[0].astype(F32)).astype(WIRE)
        step[2].start()
        left = chip_sum(2, -1)
        s3[1, :112] = left[:112].astype(WIRE)
        step[1].wait_recv()
        s3[1, 112:] = (left[112:] + t2[1].astype(F32)).astype(WIRE)
        step[3].start()
        own = chip_sum(3, 0)
        for h in (0, 1):
            for g_ in range(5):
                for e in range(4):
                    gather(h, g_, e, False).wait_send()
        step[2].wait_recv()
        step[3].wait_recv()
        qp[...] = own + t3[0].astype(F32) + t3[1].astype(F32)
        owner_in = permute(qp, q, to_owner, 1)

        @pl.when(it == 0)
        def _():
            permute_wait(rows_in)
            dp[...] = rp[...]

        image, res = qp[...], rp[...]
        g[0] = mm_t(dp[...], image)
        g[1] = mm_t(res, jnp.where(it == 0, res, image))
        g[2] = mm_t(image, image)
        theirs = pl.ds(pl.multiple_of((1 - core) * HALF, HALF), HALF)
        ours = pl.ds(pl.multiple_of(core * HALF, HALF), HALF)
        swap = remote(g.at[:, theirs], gt, ar_send.at[0], ar_recv.at[0], other_core)
        swap.start()
        for i in range(4):
            core_copy(i).wait_send()
        for c_ in step:
            c_.wait_send()
        swap.wait_recv()
        g0[...] = (g[:, ours] + gt[...]).reshape(3, RING, 32, SIDE)
        pending = [swap]

        def reduce_stage(stage, source, slots, result):
            for m in range(3):
                me = here[(m + stage) % 3]
                for d in (1, 3, 2):
                    src = source.at[m, wrap(me + d)] if stage < 2 else source.at[m]
                    copy = reduce_copy(stage, m, d, src, slots.at[m, me])
                    copy.start()
                    pending.append(copy)
                slots[m, me] = source[m, me] if stage < 2 else source[m]
            for m in range(3):
                me = here[(m + stage) % 3]
                for d in (1, 3, 2):
                    slot = slots.at[m, wrap(me - d)]
                    reduce_copy(stage, m, d, slot, slot).wait_recv()
                result(m, (slots[m, 0] + slots[m, 1]) + (slots[m, 2] + slots[m, 3]))

        def put1(m, v):
            g1[m] = v.reshape(RING, 8, SIDE)

        def put2(m, v):
            g2[m] = v

        def put3(m, v):
            h1[m, here[(m + 1) % 3]] = v

        reduce_stage(0, g0, u1, put1)
        reduce_stage(1, g1, u2, put2)
        reduce_stage(2, g2, u3, put3)
        for m in range(3):
            me = here[(m + 1) % 3]
            for d in (1, 3, 2):
                copy = spread_copy(1, m, d, h1.at[m, me], h1.at[m, me])
                copy.start()
                pending.append(copy)
        for m in range(3):
            me = here[(m + 1) % 3]
            for d in (1, 3, 2):
                slot = h1.at[m, wrap(me - d)]
                spread_copy(1, m, d, slot, slot).wait_recv()
            me = here[m]
            h0[m, me] = h1[m].reshape(32, SIDE)
            for d in (1, 3, 2):
                copy = spread_copy(0, m, d, h0.at[m, me], h0.at[m, me])
                copy.start()
                pending.append(copy)
        for m in range(3):
            me = here[m]
            for d in (1, 3, 2):
                slot = h0.at[m, wrap(me - d)]
                spread_copy(0, m, d, slot, slot).wait_recv()
        gf[core] = h0[...].reshape(3, HALF, SIDE)
        join = remote(gf.at[core], gf.at[core], ar_send.at[1], ar_recv.at[1], other_core)
        join.start()
        pending.append(join)
        remote(gf.at[1 - core], gf.at[1 - core], ar_send.at[1], ar_recv.at[1], other_core).wait_recv()
        for m in range(3):
            full[m, :HALF] = gf[0, m]
            full[m, HALF:] = gf[1, m]
        for copy in pending:
            copy.wait_send()

        first = it == 0
        norm[...] = jnp.where(first, full[1], norm[...])
        cross = jnp.where(first, full[0], full[1])
        raw = full[0]
        inv[0] = 0.5 * (raw + raw.T)
        inv[1] = norm[...]
        for m in range(2):
            work[m] = inv[m, :HALF, :HALF]

        def eliminate(half, c_):
            for m, out in enumerate(gauss_jordan([work[0], work[1]], HALF)):
                work[m] = out

            @pl.when(half == 0)
            def _():
                for m in range(2):
                    t = mm(inv[m, HALF:, :HALF], work[m])
                    tri[m] = t
                    corner = inv[m, HALF:, HALF:] - mm(t, inv[m, :HALF, HALF:])
                    inv[m, :HALF, :HALF] = work[m]
                    work[m] = corner

            return c_

        lax.fori_loop(0, 2, eliminate, 0)
        for m in range(2):
            t = tri[m]
            low = mm(work[m], t)
            inv[m, :HALF, :HALF] += mm_t(t, low)
            inv[m, HALF:, :HALF] = -low
            inv[m, :HALF, HALF:] = -low.T
            inv[m, HALF:, HALF:] = work[m]
        alpha = mm(inv[0], norm[...])
        fall = mm(cross, alpha)
        after = norm[...] - fall - fall.T + mm_t(alpha, mm(full[2], alpha))
        beta = mm(inv[1], after)
        norm[...] = after
        small[0] = alpha
        small[1] = beta

        permute_wait(owner_in)
        x_ref[...] += mm(d_ref[...], alpha)
        r_ref[...] -= mm(q[...], alpha)
        d_ref[...] = r_ref[...] + mm(d_ref[...], beta)
        return carry

    lax.fori_loop(0, ITERS, iteration, 0)


def body(covariance, right_side):
    rows, cols = covariance.shape
    piece, side = right_side.shape
    vec = jax.ShapeDtypeStruct((piece, side), F32)
    vmem = pl.BlockSpec(memory_space=pltpu.VMEM)

    def f32(*shape):
        return pltpu.VMEM(shape, F32)

    def dma(n):
        return pltpu.SemaphoreType.DMA((n,))

    return pl.pallas_call(
        kernel,
        out_shape=(vec, vec, vec),
        in_specs=[pl.BlockSpec(memory_space=pl.ANY), vmem],
        out_specs=(vmem, vmem, vmem),
        scratch_shapes=[
            pltpu.VMEM((8, piece, cols), BF16),
            pltpu.VMEM((4, 4, 2, piece // 2, side), BF16),
            f32(8, piece, side),
            pltpu.VMEM((4, piece, side), WIRE),
            pltpu.VMEM((4, piece, side), WIRE),
            pltpu.VMEM((2, piece // 2, side), WIRE),
            pltpu.VMEM((2, piece // 2, side), WIRE),
            pltpu.VMEM((2, piece, side), WIRE),
            pltpu.VMEM((2, piece, side), WIRE),
            f32(piece, side), f32(piece, side), f32(piece, side), f32(piece, side),
            f32(3, side, side), f32(3, HALF, side), f32(3, 4, 32, side), f32(3, 4, 32, side),
            f32(3, 4, 8, side), f32(3, 4, 8, side), f32(3, 8, side), f32(3, 4, 8, side),
            f32(3, 4, 8, side), f32(3, 4, 32, side), f32(2, 3, HALF, side),
            f32(side, side), f32(3, side, side), f32(2, side, side),
            f32(2, HALF, HALF), f32(2, HALF, HALF), f32(2, side, side),
            pltpu.SemaphoreType.DMA,
            dma(40), dma(40), dma(8), dma(8), dma(2), dma(2), dma(56), dma(56),
        ],
        compiler_params=pltpu.CompilerParams(
            collective_id=0, has_side_effects=True, vmem_limit_bytes=60 * 1024 * 1024
        ),
    )(covariance.reshape(8, piece, cols), right_side)


def solution(mesh):
    spec = P(("col", "row"), None)
    return jax.shard_map(
        body,
        mesh=mesh,
        in_specs=(P("row", "col"), spec),
        out_specs=(spec, spec, spec),
        check_vma=False,
    )
```

time: 1710 us -> 309 us (0.18)
  waiting for transfers between devices: 1220 us -> 0 us
  other arithmetic: 337 us -> 0 us
  Pallas kernels: 0 us -> 303 us
  matrix products: 68.1 us -> 0 us
  local copies, waits for them, and re-layouts: 45.5 us -> 4.92 us
  between operations: 22.9 us -> 0.64 us
    psum x9 -> x0, waiting for transfers between devices: 940 us -> none  [the longest x6 758 us: gram_total(): return lax.psum((pieces[0],), ('row', 'col'))]
    another operation x53 -> x0, other arithmetic: 325 us -> none  [the longest x40 206 us: solve_spd(): factor = jnp.linalg.cholesky(matrix)]
    pallas_call x0 -> x1, Pallas kernels: none -> 303 us  [body(): pl.pallas_call(kernel, out_shape=(vec, vec, vec), in_specs=[pl.BlockSpec(...]
    unnamed x18 -> x0, waiting for transfers between devices: 155 us -> none
    all_gather x3 -> x0, waiting for transfers between devices: 130 us -> none  [body(): column_rows = lax.all_gather(lowered, 'row', axis=0, tiled=True)]
    dot_general x19 -> x0, matrix products: 48.9 us -> none  [the longest x3 30.9 us: body(): lax.dot_general(covariance, own_rows, (((0,), (0,)), ((), ())), preferred...]
    another operation x55 -> x0, local copies, waits for them, and re-layouts: 24.2 us -> none  [the longest x43 24 us: solve_spd(): return jax.scipy.linalg.cho_solve((factor, True), rhs_block)]
    another operation x48 -> x0, matrix products: 19.2 us -> none  [the longest x36 16.3 us: solve_spd(): return jax.scipy.linalg.cho_solve((factor, True), rhs_block)]
  transfers between devices with their start and end apart: 15 -> 0, of which waited for: 15 -> 0; matrix products, arithmetic and copies ran while one was open for 11% -> 0% of each run, Pallas kernels for 0% -> 0%
where the time goes in v1:
time: 309 us
  Pallas kernels  303 us (98%)
  local copies, waits for them, and re-layouts  4.92 us (2%)
    pallas_call x1, Pallas kernels, body(): pl.pallas_call(kernel, out_shape=(vec, vec, vec), in_specs=[pl.BlockSpec(...  303 us

profile of v1, /device:TPU:1, one launch (start us, length us, event | category | flops | bytes accessed | tf_op | source)
XLA Modules:
  0.0 308.8 jit_solution(5182151679957483812)
XLA Ops:
  0.6 303.2 %shard_map.49 = (f32[224,256]{1,0:T(8,128)}, f32[224,256]{1,0:T(8,128)}, f32[224,256]{1,0:T(8,128)}) custom-call(bf16[8,224,3584]{2,1,0:T(8,128)(2,1)} %bitcast.1, f32[224,256]{1,0:T(8,128)} %b_ref.1), custom_call_target="tpu_custom_call" | custom-call | tf_op jit(solution)/shard_map/pallas_call | solution.py:435
  303.9 1.6 copy.8
  305.5 1.6 copy.9
  307.1 1.6 copy.10

commit v2 on v1

--- a/solution.py
+++ b/solution.py
@@ -29,24 +29,56 @@
     )
 
 
-def gauss_jordan(mats, size):
-    row = lax.broadcasted_iota(jnp.int32, (size, 1), 0)
-    lane = lax.broadcasted_iota(jnp.int32, (1, size), 1)
-    mats = list(mats)
-    for k in range(size):
-        for i, m in enumerate(mats):
-            inv = 1.0 / m[k : k + 1, k : k + 1]
-            pivot_row = jnp.where(lane == k, 1.0, m[k : k + 1, :]) * inv
-            pivot_col = jnp.where(row == k, -1.0, m[:, k : k + 1])
-            rest = jnp.where((row == k) | (lane == k), 0.0, m)
-            mats[i] = rest - pivot_col * pivot_row
-    return mats
+def eliminate(mat, size):
+    sub = lax.broadcasted_iota(jnp.int32, (8, size), 0)
+    lane = lax.broadcasted_iota(jnp.int32, (8, size), 1)
+    tiles = [mat[8 * t : 8 * t + 8, :] for t in range(size // 8)]
+    for k in range(0, size, 4):
+        p, o = k // 8, k % 8
+        inside = (lane >= k) & (lane < k + 4)
+        col = [[jnp.broadcast_to(v[:, k + j : k + j + 1], (8, size)) for j in range(4)] for v in tiles]
+        e = [[col[p][j][o + i : o + i + 1, :] for j in range(4)] for i in range(4)]
+        r = [
+            jnp.where(lane[:1] == k + j, 1.0, jnp.where(inside[:1], 0.0, tiles[p][o + j : o + j + 1, :]))
+            for j in range(4)
+        ]
+        a0, a1, a2 = e[0][0], e[0][1], e[1][1]
+        da = 1.0 / (a0 * a2 - a1 * a1)
+        u = [
+            [a2 * e[0][2] - a1 * e[1][2], a2 * e[0][3] - a1 * e[1][3]],
+            [a0 * e[1][2] - a1 * e[0][2], a0 * e[1][3] - a1 * e[0][3]],
+        ]
+        s0 = e[2][2] - (e[0][2] * u[0][0] + e[1][2] * u[1][0]) * da
+        s1 = e[2][3] - (e[0][2] * u[0][1] + e[1][2] * u[1][1]) * da
+        s2 = e[3][3] - (e[0][3] * u[0][1] + e[1][3] * u[1][1]) * da
+        t = [[v * da for v in w] for w in u]
+        ds = 1.0 / (s0 * s2 - s1 * s1)
+        w0 = r[2] - t[0][0] * r[0] - t[1][0] * r[1]
+        w1 = r[3] - t[0][1] * r[0] - t[1][1] * r[1]
+        q0 = (a2 * r[0] - a1 * r[1]) * da
+        q1 = (a0 * r[1] - a1 * r[0]) * da
+        b0 = (s2 * w0 - s1 * w1) * ds
+        b1 = (s0 * w1 - s1 * w0) * ds
+        rows = [q0 - (t[0][0] * b0 + t[0][1] * b1), q1 - (t[1][0] * b0 + t[1][1] * b1), b0, b1]
+        rows = [jnp.broadcast_to(v, (8, size)) for v in rows]
+        new = []
+        for i, v in enumerate(tiles):
+            c = col[i]
+            if i == p:
+                band = (sub >= o) & (sub < o + 4)
+                c = [jnp.where(band, jnp.where(sub == o + j, -1.0, 0.0), c[j]) for j in range(4)]
+                v = jnp.where(inside | band, 0.0, v)
+            else:
+                v = jnp.where(inside, 0.0, v)
+            new.append((v - c[0] * rows[0] - c[1] * rows[1]) - (c[2] * rows[2] + c[3] * rows[3]))
+        tiles = new
+    return jnp.concatenate(tiles, axis=0)
 
 
 def kernel(
     a_hbm, b_ref, x_ref, r_ref, d_ref,
-    a, lb, part, s1, t1, s2, t2, s3, t3, rp, dp, qp, q,
-    g, gt, g0, u1, g1, u2, g2, u3, h1, h0, gf, norm, full, inv, work, tri, small,
+    a, lb, part, t1, s3, t3, rp, dp, qp, q, dold,
+    g, gt, g0, u1, g1, u2, g2, u3, h1, h0, gf, norm, full, inv, mat, work, tri, small,
     a_sem, ag_send, ag_recv, rs_send, rs_recv, pm_send, pm_recv, ar_send, ar_recv,
 ):
     row, col = lax.axis_index("row"), lax.axis_index("col")
@@ -117,37 +149,33 @@
         def _():
             copy.wait_send()
 
-    rows_in = permute(b_ref, rp, to_rows, 0)
+    rows_in = remote(b_ref, rp, pm_send.at[0], pm_recv.at[0], to_rows)
 
     r_ref[...] = b_ref[...]
     d_ref[...] = b_ref[...]
     x_ref[...] = jnp.zeros_like(x_ref)
 
-    def region(h, c1, c2, rows):
+    def region(h, c1, c2):
         zc, yc = (c2, c1) if h == 0 else (c1, c2)
-        return lb.at[zc, yc, h, rows]
+        return lb.at[zc, yc, h]
 
     def gather(h, g_, e, incoming):
         axes = (1, 2) if h == 0 else (2, 1)
         mine = (here[axes[0]], here[axes[1]])
-        if incoming:
-            off = (-1, 1, 2, 2)[e]
-        else:
-            off = (0, 0, -1, 1)[e]
-        rows = (pl.ds(0, 112), pl.ds(0, 112), pl.ds(0, 64), pl.ds(64, 48))[e]
+        off = (-1, 1, 2)[e] if incoming else 0
         if g_ == 0:
             c1, c2, axis = wrap(mine[0] + off), mine[1], axes[0]
         else:
             c1, c2, axis = wrap(mine[0] + OFFS[g_ - 1]), wrap(mine[1] + off), axes[1]
-        ref = region(h, c1, c2, rows)
-        n = h * 20 + g_ * 4 + e
-        return remote(ref, ref, ag_send.at[n], ag_recv.at[n], along(axis, 1 if e % 2 == 0 else -1))
-
-    def send(h, g_, *es):
-        for e in es:
+        ref = region(h, c1, c2)
+        n = h * 15 + g_ * 3 + e
+        return remote(ref, ref, ag_send.at[n], ag_recv.at[n], along(axis, (1, -1, 2)[e]))
+
+    def send(h, g_):
+        for e in range(3):
             gather(h, g_, e, False).start()
 
-    def take(h, g_, *es):
+    def take(h, g_, es=(0, 1, 2)):
         for e in es:
             gather(h, g_, e, True).wait_recv()
 
@@ -167,11 +195,17 @@
 
         lax.fori_loop(0, 8, body, 0)
 
+    def shift(i):
+        if isinstance(i, int):
+            return (2, 1, -1, 0)[i]
+        return jnp.where(i == 0, 2, jnp.where(i == 1, 1, jnp.where(i == 2, -1, 0)))
+
     def core_copy(i):
-        return remote(s1.at[i], t1.at[i], rs_send.at[i], rs_recv.at[i], other_core)
-
-    def ring_copy(src, dst, n, d):
-        return remote(src, dst, rs_send.at[n], rs_recv.at[n], along(0, d))
+        j = 2 * wrap(x + shift(i)) + 1 - core
+        return remote(part.at[j], t1.at[i], rs_send.at[i], rs_recv.at[i], other_core)
+
+    def ring_copy(i):
+        return remote(s3.at[i], t3.at[i], rs_send.at[4 + i], rs_recv.at[4 + i], along(0, shift(i)))
 
     def reduce_copy(stage, m, d, src, dst):
         axis = (m + stage) % 3
@@ -186,108 +220,72 @@
     def iteration(it, carry):
         lb[z, y] = d_ref[...].astype(BF16).reshape(2, 112, SIDE)
         for h in (0, 1):
-            send(h, 0, 0, 1)
-            send(h, 1, 0, 1)
+            send(h, 0)
+            send(h, 1)
 
         @pl.when(it > 0)
         def _():
             rp[...] = rp[...] - mm(qp[...], small[0])
             dp[...] = rp[...] + mm(dp[...], small[1])
 
-        for h in (0, 1):
-            take(h, 0, 0)
-            send(h, 0, 2)
-            send(h, 2, 0, 1)
-        for h in (0, 1):
-            take(h, 0, 1)
-            send(h, 0, 3)
-            send(h, 3, 0, 1)
-        for h in (0, 1):
-            take(h, 1, 0)
-            send(h, 1, 2)
-            take(h, 1, 1)
-            send(h, 1, 3)
-        for h in (0, 1):
-            take(h, 0, 2, 3)
-            send(h, 4, 0, 1)
+        for k in range(3):
+            for h in (0, 1):
+                take(h, 0, (k,))
+                send(h, k + 2)
 
         @pl.when(it == 0)
         def _():
+            @pl.when(jnp.logical_not(fixed))
+            def _():
+                rows_in.start()
+
+            @pl.when(fixed)
+            def _():
+                pltpu.make_async_copy(b_ref, rp, pm_recv.at[0]).start()
+
             load_a.wait()
 
-        for h in (0, 1):
-            take(h, 2, 0)
-            send(h, 2, 2)
-            take(h, 2, 1)
-            send(h, 2, 3)
-        take(1, 1, 2, 3)
+        @pl.when(it > 0)
+        def _():
+            x_ref[...] += mm(dold[...], small[0])
+
+        take(1, 1)
         all_products(z, True)
-        for h in (0, 1):
-            take(h, 3, 0)
-            send(h, 3, 2)
-            take(h, 3, 1)
-            send(h, 3, 3)
-        for h in (0, 1):
-            take(h, 4, 0)
-            send(h, 4, 2)
-            take(h, 4, 1)
-            send(h, 4, 3)
-        take(1, 2, 2, 3)
-        all_products(wrap(z - 1), False)
-        take(1, 3, 2, 3)
-        all_products(wrap(z + 1), False)
-        take(1, 4, 2, 3)
+        for k in (1, 2):
+            for g_ in (1, 2, 3, 4):
+                take(0, g_, (k - 1,))
+            take(1, k + 1)
+            all_products(wrap(z + OFFS[k]), False)
         for g_ in (1, 2, 3, 4):
-            take(0, g_, 2, 3)
+            take(0, g_, (2,))
+        take(1, 4)
 
         last = wrap(z + 2)
 
         def finish(i, c_):
-            off = jnp.where(i == 0, 2, jnp.where(i == 1, 1, jnp.where(i == 2, 3, 0)))
-            xc = (x + off) % RING
-            j = 2 * xc + 1 - core
+            j = 2 * wrap(x + shift(i)) + 1 - core
             product(last, j, False)
-            s1[i] = part[j].astype(WIRE)
             core_copy(i).start()
-            product(last, 2 * xc + core, False)
+            product(last, 2 * wrap(x + shift(i)) + core, False)
             return c_
 
         lax.fori_loop(0, 4, finish, 0)
 
-        def chip_sum(i, off):
+        def chip_sum(i):
             core_copy(i).wait_recv()
-            return part[2 * wrap(x + off) + core] + t1[i].astype(F32)
-
-        far = chip_sum(0, 2)
-        s2[0] = far[:112].astype(WIRE)
-        s2[1] = far[112:].astype(WIRE)
-        step = [
-            ring_copy(s2.at[0], t2.at[0], 4, 1),
-            ring_copy(s2.at[1], t2.at[1], 5, -1),
-            ring_copy(s3.at[0], t3.at[0], 6, 1),
-            ring_copy(s3.at[1], t3.at[1], 7, -1),
-        ]
-        step[0].start()
-        step[1].start()
-        right = chip_sum(1, 1)
-        s3[0, 112:] = right[112:].astype(WIRE)
-        step[0].wait_recv()
-        s3[0, :112] = (right[:112] + t2[0].astype(F32)).astype(WIRE)
-        step[2].start()
-        left = chip_sum(2, -1)
-        s3[1, :112] = left[:112].astype(WIRE)
-        step[1].wait_recv()
-        s3[1, 112:] = (left[112:] + t2[1].astype(F32)).astype(WIRE)
-        step[3].start()
-        own = chip_sum(3, 0)
+            return part[2 * wrap(x + shift(i)) + core] + t1[i]
+
+        for i in range(3):
+            s3[i] = chip_sum(i).astype(WIRE)
+            ring_copy(i).start()
+        own = chip_sum(3)
         for h in (0, 1):
             for g_ in range(5):
-                for e in range(4):
+                for e in range(3):
                     gather(h, g_, e, False).wait_send()
-        step[2].wait_recv()
-        step[3].wait_recv()
-        qp[...] = own + t3[0].astype(F32) + t3[1].astype(F32)
-        owner_in = permute(qp, q, to_owner, 1)
+        for i in range(3):
+            ring_copy(i).wait_recv()
+        qp[...] = own + (t3[0].astype(F32) + t3[1].astype(F32) + t3[2].astype(F32))
 
         @pl.when(it == 0)
         def _():
@@ -304,8 +302,8 @@
         swap.start()
         for i in range(4):
             core_copy(i).wait_send()
-        for c_ in step:
-            c_.wait_send()
+        for i in range(3):
+            ring_copy(i).wait_send()
         swap.wait_recv()
         g0[...] = (g[:, ours] + gt[...]).reshape(3, RING, 32, SIDE)
         pending = [swap]
@@ -371,38 +369,38 @@
         for copy in pending:
             copy.wait_send()
 
+        owner_in = permute(qp, q, to_owner, 1)
+
         first = it == 0
         norm[...] = jnp.where(first, full[1], norm[...])
         cross = jnp.where(first, full[0], full[1])
         raw = full[0]
-        inv[0] = 0.5 * (raw + raw.T)
-        inv[1] = norm[...]
-        for m in range(2):
-            work[m] = inv[m, :HALF, :HALF]
-
-        def eliminate(half, c_):
-            for m, out in enumerate(gauss_jordan([work[0], work[1]], HALF)):
-                work[m] = out
+        mat[...] = jnp.where(core == 0, 0.5 * (raw + raw.T), norm[...])
+        work[...] = mat[:HALF, :HALF]
+
+        def half_step(half, c_):
+            work[...] = eliminate(work[...], HALF)
 
             @pl.when(half == 0)
             def _():
-                for m in range(2):
-                    t = mm(inv[m, HALF:, :HALF], work[m])
-                    tri[m] = t
-                    corner = inv[m, HALF:, HALF:] - mm(t, inv[m, :HALF, HALF:])
-                    inv[m, :HALF, :HALF] = work[m]
-                    work[m] = corner
+                t = mm(mat[HALF:, :HALF], work[...])
+                tri[...] = t
+                corner = mat[HALF:, HALF:] - mm(t, mat[:HALF, HALF:])
+                mat[:HALF, :HALF] = work[...]
+                work[...] = corner
 
             return c_
 
-        lax.fori_loop(0, 2, eliminate, 0)
-        for m in range(2):
-            t = tri[m]
-            low = mm(work[m], t)
-            inv[m, :HALF, :HALF] += mm_t(t, low)
-            inv[m, HALF:, :HALF] = -low
-            inv[m, :HALF, HALF:] = -low.T
-            inv[m, HALF:, HALF:] = work[m]
+        lax.fori_loop(0, 2, half_step, 0)
+        t = tri[...]
+        low = mm(work[...], t)
+        inv[core, :HALF, :HALF] = mat[:HALF, :HALF] + mm_t(t, low)
+        inv[core, HALF:, :HALF] = -low
+        inv[core, :HALF, HALF:] = -low.T
+        inv[core, HALF:, HALF:] = work[...]
+        share = remote(inv.at[core], inv.at[core], ar_send.at[56], ar_recv.at[56], other_core)
+        share.start()
+        remote(inv.at[1 - core], inv.at[1 - core], ar_send.at[56], ar_recv.at[56], other_core).wait_recv()
         alpha = mm(inv[0], norm[...])
         fall = mm(cross, alpha)
         after = norm[...] - fall - fall.T + mm_t(alpha, mm(full[2], alpha))
@@ -412,12 +410,14 @@
         small[1] = beta
 
         permute_wait(owner_in)
-        x_ref[...] += mm(d_ref[...], alpha)
         r_ref[...] -= mm(q[...], alpha)
+        dold[...] = d_ref[...]
         d_ref[...] = r_ref[...] + mm(d_ref[...], beta)
+        share.wait_send()
         return carry
 
     lax.fori_loop(0, ITERS, iteration, 0)
+    x_ref[...] += mm(dold[...], small[0])
 
 
 def body(covariance, right_side):
@@ -441,20 +441,17 @@
             pltpu.VMEM((8, piece, cols), BF16),
             pltpu.VMEM((4, 4, 2, piece // 2, side), BF16),
             f32(8, piece, side),
-            pltpu.VMEM((4, piece, side), WIRE),
-            pltpu.VMEM((4, piece, side), WIRE),
-            pltpu.VMEM((2, piece // 2, side), WIRE),
-            pltpu.VMEM((2, piece // 2, side), WIRE),
-            pltpu.VMEM((2, piece, side), WIRE),
-            pltpu.VMEM((2, piece, side), WIRE),
-            f32(piece, side), f32(piece, side), f32(piece, side), f32(piece, side),
+            f32(4, piece, side),
+            pltpu.VMEM((3, piece, side), WIRE),
+            pltpu.VMEM((3, piece, side), WIRE),
+            f32(piece, side), f32(piece, side), f32(piece, side), f32(piece, side), f32(piece, side),
             f32(3, side, side), f32(3, HALF, side), f32(3, 4, 32, side), f32(3, 4, 32, side),
             f32(3, 4, 8, side), f32(3, 4, 8, side), f32(3, 8, side), f32(3, 4, 8, side),
             f32(3, 4, 8, side), f32(3, 4, 32, side), f32(2, 3, HALF, side),
             f32(side, side), f32(3, side, side), f32(2, side, side),
-            f32(2, HALF, HALF), f32(2, HALF, HALF), f32(2, side, side),
+            f32(side, side), f32(HALF, HALF), f32(HALF, HALF), f32(2, side, side),
             pltpu.SemaphoreType.DMA,
-            dma(40), dma(40), dma(8), dma(8), dma(2), dma(2), dma(56), dma(56),
+            dma(30), dma(30), dma(7), dma(7), dma(2), dma(2), dma(57), dma(57),
         ],
         compiler_params=pltpu.CompilerParams(
             collective_id=0, has_side_effects=True, vmem_limit_bytes=60 * 1024 * 1024

time: 309 us -> 233 us (0.75)
  Pallas kernels: 303 us -> 227 us
    pallas_call x1, Pallas kernels: 303 us -> 227 us  [body(): pl.pallas_call(kernel, out_shape=(vec, vec, vec), in_specs=[pl.BlockSpec(...]
where the time goes in v2:
time: 233 us
  Pallas kernels  227 us (97%)
  local copies, waits for them, and re-layouts  4.92 us (2%)
    pallas_call x1, Pallas kernels, body(): pl.pallas_call(kernel, out_shape=(vec, vec, vec), in_specs=[pl.BlockSpec(...  227 us
    unnamed x3, local copies, waits for them, and re-layouts  4.92 us

profile of v2, /device:TPU:1, one launch (start us, length us, event | category | flops | bytes accessed | tf_op | source)
XLA Modules:
  0.0 232.9 jit_solution(16952346108152828039)
XLA Ops:
  0.6 227.3 %shard_map.49 = (f32[224,256]{1,0:T(8,128)}, f32[224,256]{1,0:T(8,128)}, f32[224,256]{1,0:T(8,128)}) custom-call(bf16[8,224,3584]{2,1,0:T(8,128)(2,1)} %bitcast.1, f32[224,256]{1,0:T(8,128)} %b_ref.1), custom_call_target="tpu_custom_call" | custom-call | tf_op jit(solution)/shard_map/pallas_call | solution.py:435
  227.9 1.6 copy.8
  229.6 1.6 copy.9
  231.2 1.6 copy.10

commit v3 on v2

--- a/solution.py
+++ b/solution.py
@@ -78,7 +78,7 @@
 def kernel(
     a_hbm, b_ref, x_ref, r_ref, d_ref,
     a, lb, part, t1, s3, t3, rp, dp, qp, q, dold,
-    g, gt, g0, u1, g1, u2, g2, u3, h1, h0, gf, norm, full, inv, mat, work, tri, small,
+    g, gt, g0, u1, g2, u3, h0, gf, norm, full, inv, mat, work, tri, small,
     a_sem, ag_send, ag_recv, rs_send, rs_recv, pm_send, pm_recv, ar_send, ar_recv,
 ):
     row, col = lax.axis_index("row"), lax.axis_index("col")
@@ -98,6 +98,12 @@
 
     other_core = device(here, 1 - core)
 
+    def in_plane(m, d, f):
+        pos = list(here)
+        pos[m] = wrap(pos[m] + d)
+        pos[(m + 1) % 3] = wrap(pos[(m + 1) % 3] + f)
+        return device(pos, core)
+
     def remote(src, dst, send, recv, target):
         return pltpu.make_async_remote_copy(
             src_ref=src, dst_ref=dst, send_sem=send, recv_sem=recv, device_id=target, device_id_type=MESH
@@ -121,13 +127,17 @@
         for d in range(1, RING):
             greet(along(axis, d))
     greet(other_core)
+    for m in range(3):
+        for d in range(1, RING):
+            for f in range(1, RING):
+                greet(in_plane(m, d, f))
 
     @pl.when(jnp.logical_not(fixed))
     def _():
         greet(to_rows)
         greet(to_owner)
 
-    pl.semaphore_wait(barrier, jnp.where(fixed, 10, 12))
+    pl.semaphore_wait(barrier, jnp.where(fixed, 37, 39))
 
     def permute(src, dst, target, n):
         copy = remote(src, dst, pm_send.at[n], pm_recv.at[n], target)
@@ -207,21 +217,19 @@
     def ring_copy(i):
         return remote(s3.at[i], t3.at[i], rs_send.at[4 + i], rs_recv.at[4 + i], along(0, shift(i)))
 
-    def reduce_copy(stage, m, d, src, dst):
-        axis = (m + stage) % 3
-        n = 2 + (stage * 3 + m) * 3 + d - 1
-        return remote(src, dst, ar_send.at[n], ar_recv.at[n], along(axis, d))
-
-    def spread_copy(stage, m, d, src, dst):
-        axis = (m + stage) % 3
-        n = 29 + (stage * 3 + m) * 3 + d - 1
-        return remote(src, dst, ar_send.at[n], ar_recv.at[n], along(axis, d))
+    def plane_copy(base, m, k, src, dst):
+        n = base + 16 * m + k
+        return remote(src, dst, ar_send.at[n], ar_recv.at[n], in_plane(m, k // 4, k % 4))
+
+    def line_copy(m, d, src, dst):
+        n = 96 + 3 * m + d - 1
+        return remote(src, dst, ar_send.at[n], ar_recv.at[n], along((m + 2) % 3, d))
 
     def iteration(it, carry):
         lb[z, y] = d_ref[...].astype(BF16).reshape(2, 112, SIDE)
-        for h in (0, 1):
-            send(h, 0)
-            send(h, 1)
+        for g_ in (0, 1):
+            for h in (0, 1):
+                send(h, g_)
 
         @pl.when(it > 0)
         def _():
@@ -298,76 +306,75 @@
         g[2] = mm_t(image, image)
         theirs = pl.ds(pl.multiple_of((1 - core) * HALF, HALF), HALF)
         ours = pl.ds(pl.multiple_of(core * HALF, HALF), HALF)
-        swap = remote(g.at[:, theirs], gt, ar_send.at[0], ar_recv.at[0], other_core)
+        swap = remote(g.at[:, theirs], gt, ar_send.at[105], ar_recv.at[105], other_core)
         swap.start()
         for i in range(4):
             core_copy(i).wait_send()
         for i in range(3):
             ring_copy(i).wait_send()
         swap.wait_recv()
-        g0[...] = (g[:, ours] + gt[...]).reshape(3, RING, 32, SIDE)
+        g0[...] = (g[:, ours] + gt[...]).reshape(3, RING, RING, 8, SIDE)
         pending = [swap]
 
-        def reduce_stage(stage, source, slots, result):
-            for m in range(3):
-                me = here[(m + stage) % 3]
-                for d in (1, 3, 2):
-                    src = source.at[m, wrap(me + d)] if stage < 2 else source.at[m]
-                    copy = reduce_copy(stage, m, d, src, slots.at[m, me])
-                    copy.start()
-                    pending.append(copy)
-                slots[m, me] = source[m, me] if stage < 2 else source[m]
-            for m in range(3):
-                me = here[(m + stage) % 3]
-                for d in (1, 3, 2):
-                    slot = slots.at[m, wrap(me - d)]
-                    reduce_copy(stage, m, d, slot, slot).wait_recv()
-                result(m, (slots[m, 0] + slots[m, 1]) + (slots[m, 2] + slots[m, 3]))
-
-        def put1(m, v):
-            g1[m] = v.reshape(RING, 8, SIDE)
-
-        def put2(m, v):
-            g2[m] = v
-
-        def put3(m, v):
-            h1[m, here[(m + 1) % 3]] = v
-
-        reduce_stage(0, g0, u1, put1)
-        reduce_stage(1, g1, u2, put2)
-        reduce_stage(2, g2, u3, put3)
-        for m in range(3):
-            me = here[(m + 1) % 3]
+        def each(m, fn):
+            i, j = here[m], here[(m + 1) % 3]
+
+            def step(k, c_):
+                fn(k, i, j)
+                return c_
+
+            lax.fori_loop(1, 16, step, 0)
+
+        def reduce_send(m, k, i, j):
+            src = g0.at[m, wrap(i + k // 4), wrap(j + k % 4)]
+            return plane_copy(0, m, k, src, u1.at[m, i, j])
+
+        def spread_send(m, k, i, j):
+            return plane_copy(48, m, k, h0.at[m, i, j], h0.at[m, i, j])
+
+        for m in range(3):
+            each(m, lambda k, i, j: reduce_send(m, k, i, j).start())
+            i, j = here[m], here[(m + 1) % 3]
+            u1[m, i, j] = g0[m, i, j]
+        for m in range(3):
+            def arrived(k, i, j):
+                slot = u1.at[m, wrap(i - k // 4), wrap(j - k % 4)]
+                plane_copy(0, m, k, slot, slot).wait_recv()
+
+            each(m, arrived)
+            g2[m] = jnp.sum(u1[m].reshape(16, 8, SIDE), axis=0)
+            me = here[(m + 2) % 3]
             for d in (1, 3, 2):
-                copy = spread_copy(1, m, d, h1.at[m, me], h1.at[m, me])
+                copy = line_copy(m, d, g2.at[m], u3.at[m, me])
                 copy.start()
                 pending.append(copy)
-        for m in range(3):
-            me = here[(m + 1) % 3]
+            u3[m, me] = g2[m]
+        for m in range(3):
+            me = here[(m + 2) % 3]
             for d in (1, 3, 2):
-                slot = h1.at[m, wrap(me - d)]
-                spread_copy(1, m, d, slot, slot).wait_recv()
-            me = here[m]
-            h0[m, me] = h1[m].reshape(32, SIDE)
-            for d in (1, 3, 2):
-                copy = spread_copy(0, m, d, h0.at[m, me], h0.at[m, me])
-                copy.start()
-                pending.append(copy)
-        for m in range(3):
-            me = here[m]
-            for d in (1, 3, 2):
-                slot = h0.at[m, wrap(me - d)]
-                spread_copy(0, m, d, slot, slot).wait_recv()
+                slot = u3.at[m, wrap(me - d)]
+                line_copy(m, d, slot, slot).wait_recv()
+            h0[m, here[m], here[(m + 1) % 3]] = (u3[m, 0] + u3[m, 1]) + (u3[m, 2] + u3[m, 3])
+            each(m, lambda k, i, j: spread_send(m, k, i, j).start())
+        for m in range(3):
+            def landed(k, i, j):
+                slot = h0.at[m, wrap(i - k // 4), wrap(j - k % 4)]
+                plane_copy(48, m, k, slot, slot).wait_recv()
+
+            each(m, landed)
         gf[core] = h0[...].reshape(3, HALF, SIDE)
-        join = remote(gf.at[core], gf.at[core], ar_send.at[1], ar_recv.at[1], other_core)
+        join = remote(gf.at[core], gf.at[core], ar_send.at[106], ar_recv.at[106], other_core)
         join.start()
         pending.append(join)
-        remote(gf.at[1 - core], gf.at[1 - core], ar_send.at[1], ar_recv.at[1], other_core).wait_recv()
+        remote(gf.at[1 - core], gf.at[1 - core], ar_send.at[106], ar_recv.at[106], other_core).wait_recv()
         for m in range(3):
             full[m, :HALF] = gf[0, m]
             full[m, HALF:] = gf[1, m]
         for copy in pending:
             copy.wait_send()
+        for m in range(3):
+            each(m, lambda k, i, j: reduce_send(m, k, i, j).wait_send())
+            each(m, lambda k, i, j: spread_send(m, k, i, j).wait_send())
 
         owner_in = permute(qp, q, to_owner, 1)
 
@@ -398,9 +405,9 @@
         inv[core, HALF:, :HALF] = -low
         inv[core, :HALF, HALF:] = -low.T
         inv[core, HALF:, HALF:] = work[...]
-        share = remote(inv.at[core], inv.at[core], ar_send.at[56], ar_recv.at[56], other_core)
+        share = remote(inv.at[core], inv.at[core], ar_send.at[107], ar_recv.at[107], other_core)
         share.start()
-        remote(inv.at[1 - core], inv.at[1 - core], ar_send.at[56], ar_recv.at[56], other_core).wait_recv()
+        remote(inv.at[1 - core], inv.at[1 - core], ar_send.at[107], ar_recv.at[107], other_core).wait_recv()
         alpha = mm(inv[0], norm[...])
         fall = mm(cross, alpha)
         after = norm[...] - fall - fall.T + mm_t(alpha, mm(full[2], alpha))
@@ -432,7 +439,7 @@
     def dma(n):
         return pltpu.SemaphoreType.DMA((n,))
 
-    return pl.pallas_call(
+    out = pl.pallas_call(
         kernel,
         out_shape=(vec, vec, vec),
         in_specs=[pl.BlockSpec(memory_space=pl.ANY), vmem],
@@ -445,18 +452,23 @@
             pltpu.VMEM((3, piece, side), WIRE),
             pltpu.VMEM((3, piece, side), WIRE),
             f32(piece, side), f32(piece, side), f32(piece, side), f32(piece, side), f32(piece, side),
-            f32(3, side, side), f32(3, HALF, side), f32(3, 4, 32, side), f32(3, 4, 32, side),
-            f32(3, 4, 8, side), f32(3, 4, 8, side), f32(3, 8, side), f32(3, 4, 8, side),
-            f32(3, 4, 8, side), f32(3, 4, 32, side), f32(2, 3, HALF, side),
+            f32(3, side, side), f32(3, HALF, side), f32(3, 4, 4, 8, side), f32(3, 4, 4, 8, side),
+            f32(3, 8, side), f32(3, 4, 8, side), f32(3, 4, 4, 8, side), f32(2, 3, HALF, side),
             f32(side, side), f32(3, side, side), f32(2, side, side),
             f32(side, side), f32(HALF, HALF), f32(HALF, HALF), f32(2, side, side),
             pltpu.SemaphoreType.DMA,
-            dma(30), dma(30), dma(7), dma(7), dma(2), dma(2), dma(57), dma(57),
+            dma(30), dma(30), dma(7), dma(7), dma(2), dma(2), dma(108), dma(108),
         ],
         compiler_params=pltpu.CompilerParams(
             collective_id=0, has_side_effects=True, vmem_limit_bytes=60 * 1024 * 1024
         ),
     )(covariance.reshape(8, piece, cols), right_side)
+
+    def hand_over(*refs):
+        for src, dst in zip(refs[:3], refs[3:]):
+            dst[...] = src[...]
+
+    return pl.pallas_call(hand_over, out_shape=(vec, vec, vec))(*out)
 
 
 def solution(mesh):

time: 233 us -> 222 us (0.953)
  Pallas kernels: 227 us -> 221 us
  local copies, waits for them, and re-layouts: 4.92 us -> 0 us
    pallas_call x1, Pallas kernels: 227 us -> 219 us  [body(): pl.pallas_call(kernel, out_shape=(vec, vec, vec), in_specs=[pl.BlockSpec(...]
    unnamed x3 -> x0, local copies, waits for them, and re-layouts: 4.92 us -> none
where the time goes in v3:
time: 222 us
  Pallas kernels  221 us (100%)
    pallas_call x1, Pallas kernels, body(): pl.pallas_call(kernel, out_shape=(vec, vec, vec), in_specs=[pl.BlockSpec(...  219 us

profile of v3, /device:TPU:1, one launch (start us, length us, event | category | flops | bytes accessed | tf_op | source)
XLA Modules:
  0.0 221.7 jit_solution(3550399816290483119)
XLA Ops:
  0.6 219.0 %shard_map.49 = (f32[224,256]{1,0:T(8,128)}, f32[224,256]{1,0:T(8,128)}, f32[224,256]{1,0:T(8,128)}) custom-call(bf16[8,224,3584]{2,1,0:T(8,128)(2,1)} %bitcast.1, f32[224,256]{1,0:T(8,128)} %b_ref.1), custom_call_target="tpu_custom_call" | custom-call | tf_op jit(solution)/shard_map/pallas_call | solution.py:442
  219.7 2.0 shard_map.50

commit v4 on v3

--- a/solution.py
+++ b/solution.py
@@ -33,15 +33,18 @@
     sub = lax.broadcasted_iota(jnp.int32, (8, size), 0)
     lane = lax.broadcasted_iota(jnp.int32, (8, size), 1)
     tiles = [mat[8 * t : 8 * t + 8, :] for t in range(size // 8)]
+    lower, scaled = [], []
     for k in range(0, size, 4):
         p, o = k // 8, k % 8
         inside = (lane >= k) & (lane < k + 4)
-        col = [[jnp.broadcast_to(v[:, k + j : k + j + 1], (8, size)) for j in range(4)] for v in tiles]
+        live = range(p if o == 0 else p + 1, size // 8)
+        col = {
+            i: [jnp.broadcast_to(tiles[i][:, k + j : k + j + 1], (8, size)) for j in range(4)]
+            for i in sorted({p, *live})
+        }
         e = [[col[p][j][o + i : o + i + 1, :] for j in range(4)] for i in range(4)]
-        r = [
-            jnp.where(lane[:1] == k + j, 1.0, jnp.where(inside[:1], 0.0, tiles[p][o + j : o + j + 1, :]))
-            for j in range(4)
-        ]
+        pivot = jnp.where(inside, jnp.where(lane - k == sub - o, 1.0, 0.0), tiles[p])
+        r = [pivot[o + j : o + j + 1, :] for j in range(4)]
         a0, a1, a2 = e[0][0], e[0][1], e[1][1]
         da = 1.0 / (a0 * a2 - a1 * a1)
         u = [
@@ -61,18 +64,19 @@
         b1 = (s0 * w1 - s1 * w0) * ds
         rows = [q0 - (t[0][0] * b0 + t[0][1] * b1), q1 - (t[1][0] * b0 + t[1][1] * b1), b0, b1]
         rows = [jnp.broadcast_to(v, (8, size)) for v in rows]
-        new = []
-        for i, v in enumerate(tiles):
-            c = col[i]
-            if i == p:
-                band = (sub >= o) & (sub < o + 4)
-                c = [jnp.where(band, jnp.where(sub == o + j, -1.0, 0.0), c[j]) for j in range(4)]
-                v = jnp.where(inside | band, 0.0, v)
-            else:
-                v = jnp.where(inside, 0.0, v)
-            new.append((v - c[0] * rows[0] - c[1] * rows[1]) - (c[2] * rows[2] + c[3] * rows[3]))
-        tiles = new
-    return jnp.concatenate(tiles, axis=0)
+        left = lane < k + 4
+        piece = jnp.where(sub == o, rows[0], jnp.where(sub == o + 1, rows[1], jnp.where(sub == o + 2, rows[2], rows[3])))
+        pivot, piece = jnp.where(left, pivot, 0.0), jnp.where(left, piece, 0.0)
+        if o == 0:
+            lower.append(pivot)
+            scaled.append(piece)
+        else:
+            lower[p] = jnp.where(sub < 4, lower[p], pivot)
+            scaled[p] = jnp.where(sub < 4, scaled[p], piece)
+        for i in live:
+            c, v = col[i], jnp.where(inside, 0.0, tiles[i])
+            tiles[i] = (v - c[0] * rows[0] - c[1] * rows[1]) - (c[2] * rows[2] + c[3] * rows[3])
+    return mm_t(jnp.concatenate(lower, axis=0), jnp.concatenate(scaled, axis=0))
 
 
 def kernel(
@@ -356,58 +360,65 @@
                 line_copy(m, d, slot, slot).wait_recv()
             h0[m, here[m], here[(m + 1) % 3]] = (u3[m, 0] + u3[m, 1]) + (u3[m, 2] + u3[m, 3])
             each(m, lambda k, i, j: spread_send(m, k, i, j).start())
-        for m in range(3):
+        owner_in = permute(qp, q, to_owner, 1)
+
+        def join(m, half):
+            return remote(gf.at[half, m], gf.at[half, m], ar_send.at[107 + m], ar_recv.at[107 + m], other_core)
+
+        def land(m):
             def landed(k, i, j):
                 slot = h0.at[m, wrap(i - k // 4), wrap(j - k % 4)]
                 plane_copy(48, m, k, slot, slot).wait_recv()
 
             each(m, landed)
-        gf[core] = h0[...].reshape(3, HALF, SIDE)
-        join = remote(gf.at[core], gf.at[core], ar_send.at[106], ar_recv.at[106], other_core)
-        join.start()
-        pending.append(join)
-        remote(gf.at[1 - core], gf.at[1 - core], ar_send.at[106], ar_recv.at[106], other_core).wait_recv()
-        for m in range(3):
+            gf[core, m] = h0[m].reshape(HALF, SIDE)
+            join(m, core).start()
+
+        def joined(m):
+            join(m, 1 - core).wait_recv()
             full[m, :HALF] = gf[0, m]
             full[m, HALF:] = gf[1, m]
+
+        first = it == 0
+        later = it > 0
+        land(0)
+        pl.when(first)(lambda: land(1))
+        joined(0)
+
+        @pl.when(first)
+        def _():
+            joined(1)
+            norm[...] = full[1]
+
+        raw = full[0]
+        mat[...] = jnp.where(core == 0, 0.5 * (raw + raw.T), norm[...])
+        head = eliminate(mat[:HALF, :HALF], HALF)
+        t = mm(mat[HALF:, :HALF], head)
+        corner = mat[HALF:, HALF:] - mm(t, mat[:HALF, HALF:])
+        tri[...] = t
+        work[...] = corner
+        mat[:HALF, :HALF] = head
+        pl.when(later)(lambda: land(1))
+        land(2)
+        tail = eliminate(work[...], HALF)
+        t = tri[...]
+        low = mm(tail, t)
+        inv[core, :HALF, :HALF] = mat[:HALF, :HALF] + mm_t(t, low)
+        inv[core, HALF:, :HALF] = -low
+        inv[core, :HALF, HALF:] = -low.T
+        inv[core, HALF:, HALF:] = tail
+        share = remote(inv.at[core], inv.at[core], ar_send.at[106], ar_recv.at[106], other_core)
+        share.start()
+        pl.when(later)(lambda: joined(1))
+        joined(2)
+        cross = jnp.where(first, full[0], full[1])
         for copy in pending:
             copy.wait_send()
         for m in range(3):
+            join(m, core).wait_send()
             each(m, lambda k, i, j: reduce_send(m, k, i, j).wait_send())
             each(m, lambda k, i, j: spread_send(m, k, i, j).wait_send())
-
-        owner_in = permute(qp, q, to_owner, 1)
-
-        first = it == 0
-        norm[...] = jnp.where(first, full[1], norm[...])
-        cross = jnp.where(first, full[0], full[1])
-        raw = full[0]
-        mat[...] = jnp.where(core == 0, 0.5 * (raw + raw.T), norm[...])
-        work[...] = mat[:HALF, :HALF]
-
-        def half_step(half, c_):
-            work[...] = eliminate(work[...], HALF)
-
-            @pl.when(half == 0)
-            def _():
-                t = mm(mat[HALF:, :HALF], work[...])
-                tri[...] = t
-                corner = mat[HALF:, HALF:] - mm(t, mat[:HALF, HALF:])
-                mat[:HALF, :HALF] = work[...]
-                work[...] = corner
-
-            return c_
-
-        lax.fori_loop(0, 2, half_step, 0)
-        t = tri[...]
-        low = mm(work[...], t)
-        inv[core, :HALF, :HALF] = mat[:HALF, :HALF] + mm_t(t, low)
-        inv[core, HALF:, :HALF] = -low
-        inv[core, :HALF, HALF:] = -low.T
-        inv[core, HALF:, HALF:] = work[...]
-        share = remote(inv.at[core], inv.at[core], ar_send.at[107], ar_recv.at[107], other_core)
-        share.start()
-        remote(inv.at[1 - core], inv.at[1 - core], ar_send.at[107], ar_recv.at[107], other_core).wait_recv()
+        remote(inv.at[1 - core], inv.at[1 - core], ar_send.at[106], ar_recv.at[106], other_core).wait_recv()
         alpha = mm(inv[0], norm[...])
         fall = mm(cross, alpha)
         after = norm[...] - fall - fall.T + mm_t(alpha, mm(full[2], alpha))
@@ -457,7 +468,7 @@
             f32(side, side), f32(3, side, side), f32(2, side, side),
             f32(side, side), f32(HALF, HALF), f32(HALF, HALF), f32(2, side, side),
             pltpu.SemaphoreType.DMA,
-            dma(30), dma(30), dma(7), dma(7), dma(2), dma(2), dma(108), dma(108),
+            dma(30), dma(30), dma(7), dma(7), dma(2), dma(2), dma(110), dma(110),
         ],
         compiler_params=pltpu.CompilerParams(
             collective_id=0, has_side_effects=True, vmem_limit_bytes=60 * 1024 * 1024

time: 222 us -> 222 us (level)
  no operation moved by 1% of the time
where the time goes in v4:
time: 222 us; the launch traced here: 220 us
  Pallas kernels  219 us (99%)
    pallas_call x1, Pallas kernels, body(): pl.pallas_call(kernel, out_shape=(vec, vec, vec), in_specs=[pl.BlockSpec(...  217 us

profile of v4, /device:TPU:1, one launch (start us, length us, event | category | flops | bytes accessed | tf_op | source)
XLA Modules:
  0.0 219.8 jit_solution(2817203026768932633)
XLA Ops:
  0.6 217.2 %shard_map.49 = (f32[224,256]{1,0:T(8,128)}, f32[224,256]{1,0:T(8,128)}, f32[224,256]{1,0:T(8,128)}) custom-call(bf16[8,224,3584]{2,1,0:T(8,128)(2,1)} %bitcast.1, f32[224,256]{1,0:T(8,128)} %b_ref.1), custom_call_target="tpu_custom_call" | custom-call | tf_op jit(solution)/shard_map/pallas_call | solution.py:453
  217.8 2.0 shard_map.50

commit v5 on v4

--- a/solution.py
+++ b/solution.py
@@ -143,20 +143,21 @@
 
     pl.semaphore_wait(barrier, jnp.where(fixed, 37, 39))
 
-    def permute(src, dst, target, n):
-        copy = remote(src, dst, pm_send.at[n], pm_recv.at[n], target)
-
+    def owner_copy(part_):
+        rows = pl.ds(112 * part_, 112)
+        return remote(qp.at[rows], q.at[rows], pm_send.at[1 + part_], pm_recv.at[1 + part_], to_owner)
+
+    def owner_start(part_):
         @pl.when(jnp.logical_not(fixed))
         def _():
-            copy.start()
+            owner_copy(part_).start()
 
         @pl.when(fixed)
         def _():
-            pltpu.make_async_copy(src, dst, pm_recv.at[n]).start()
-
-        return copy
-
-    def permute_wait(copy):
+            rows = pl.ds(112 * part_, 112)
+            pltpu.make_async_copy(qp.at[rows], q.at[rows], pm_recv.at[1 + part_]).start()
+
+    def settle(copy):
         copy.wait_recv()
 
         @pl.when(jnp.logical_not(fixed))
@@ -235,6 +236,7 @@
             for h in (0, 1):
                 send(h, g_)
 
+
         @pl.when(it > 0)
         def _():
             rp[...] = rp[...] - mm(qp[...], small[0])
@@ -301,7 +303,7 @@
 
         @pl.when(it == 0)
         def _():
-            permute_wait(rows_in)
+            settle(rows_in)
             dp[...] = rp[...]
 
         image, res = qp[...], rp[...]
@@ -360,7 +362,6 @@
                 line_copy(m, d, slot, slot).wait_recv()
             h0[m, here[m], here[(m + 1) % 3]] = (u3[m, 0] + u3[m, 1]) + (u3[m, 2] + u3[m, 3])
             each(m, lambda k, i, j: spread_send(m, k, i, j).start())
-        owner_in = permute(qp, q, to_owner, 1)
 
         def join(m, half):
             return remote(gf.at[half, m], gf.at[half, m], ar_send.at[107 + m], ar_recv.at[107 + m], other_core)
@@ -390,6 +391,8 @@
             joined(1)
             norm[...] = full[1]
 
+        owner_start(0)
+        owner_start(1)
         raw = full[0]
         mat[...] = jnp.where(core == 0, 0.5 * (raw + raw.T), norm[...])
         head = eliminate(mat[:HALF, :HALF], HALF)
@@ -427,7 +430,8 @@
         small[0] = alpha
         small[1] = beta
 
-        permute_wait(owner_in)
+        settle(owner_copy(0))
+        settle(owner_copy(1))
         r_ref[...] -= mm(q[...], alpha)
         dold[...] = d_ref[...]
         d_ref[...] = r_ref[...] + mm(d_ref[...], beta)
@@ -468,7 +472,7 @@
             f32(side, side), f32(3, side, side), f32(2, side, side),
             f32(side, side), f32(HALF, HALF), f32(HALF, HALF), f32(2, side, side),
             pltpu.SemaphoreType.DMA,
-            dma(30), dma(30), dma(7), dma(7), dma(2), dma(2), dma(110), dma(110),
+            dma(30), dma(30), dma(7), dma(7), dma(3), dma(3), dma(110), dma(110),
         ],
         compiler_params=pltpu.CompilerParams(
             collective_id=0, has_side_effects=True, vmem_limit_bytes=60 * 1024 * 1024

time: 222 us -> 211 us (0.950)
  Pallas kernels: 219 us -> 210 us
    pallas_call x1, Pallas kernels: 217 us -> 208 us  [body(): pl.pallas_call(kernel, out_shape=(vec, vec, vec), in_specs=[pl.BlockSpec(...]
where the time goes in v5:
time: 211 us
  Pallas kernels  210 us (100%)
    pallas_call x1, Pallas kernels, body(): pl.pallas_call(kernel, out_shape=(vec, vec, vec), in_specs=[pl.BlockSpec(...  208 us

profile of v5, /device:TPU:1, one launch (start us, length us, event | category | flops | bytes accessed | tf_op | source)
XLA Modules:
  0.0 210.7 jit_solution(12823039011483284293)
XLA Ops:
  0.6 208.1 %shard_map.49 = (f32[224,256]{1,0:T(8,128)}, f32[224,256]{1,0:T(8,128)}, f32[224,256]{1,0:T(8,128)}) custom-call(bf16[8,224,3584]{2,1,0:T(8,128)(2,1)} %bitcast.1, f32[224,256]{1,0:T(8,128)} %b_ref.1), custom_call_target="tpu_custom_call" | custom-call | tf_op jit(solution)/shard_map/pallas_call | solution.py:457
  208.7 2.0 shard_map.50

commit v6 on v5

--- a/solution.py
+++ b/solution.py
@@ -117,8 +117,9 @@
     load_a.start()
 
     piece_out = col * 16 + row
-    to_rows = (piece_out // 8, piece_out % 8)
-    piece_in = row * 8 + col
+    row_out, slot_out = piece_out // 8, piece_out % 8
+    to_rows = (row_out, 2 * wrap(slot_out // 2 + row_out // RING) + slot_out % 2)
+    piece_in = row * 8 + 2 * wrap(x - z) + core
     to_owner = (piece_in % 16, piece_in // 16)
     fixed = piece_out == piece_in
 
@@ -215,8 +216,11 @@
             return (2, 1, -1, 0)[i]
         return jnp.where(i == 0, 2, jnp.where(i == 1, 1, jnp.where(i == 2, -1, 0)))
 
+    def part_of(i):
+        return wrap(x + shift(i) - z)
+
     def core_copy(i):
-        j = 2 * wrap(x + shift(i)) + 1 - core
+        j = 2 * part_of(i) + 1 - core
         return remote(part.at[j], t1.at[i], rs_send.at[i], rs_recv.at[i], other_core)
 
     def ring_copy(i):
@@ -277,17 +281,17 @@
         last = wrap(z + 2)
 
         def finish(i, c_):
-            j = 2 * wrap(x + shift(i)) + 1 - core
+            j = 2 * part_of(i) + 1 - core
             product(last, j, False)
             core_copy(i).start()
-            product(last, 2 * wrap(x + shift(i)) + core, False)
+            product(last, 2 * part_of(i) + core, False)
             return c_
 
         lax.fori_loop(0, 4, finish, 0)
 
         def chip_sum(i):
             core_copy(i).wait_recv()
-            return part[2 * wrap(x + shift(i)) + core] + t1[i]
+            return part[2 * part_of(i) + core] + t1[i]
 
         for i in range(3):
             s3[i] = chip_sum(i).astype(WIRE)
@@ -307,20 +311,23 @@
             dp[...] = rp[...]
 
         image, res = qp[...], rp[...]
-        g[0] = mm_t(dp[...], image)
-        g[1] = mm_t(res, jnp.where(it == 0, res, image))
-        g[2] = mm_t(image, image)
         theirs = pl.ds(pl.multiple_of((1 - core) * HALF, HALF), HALF)
         ours = pl.ds(pl.multiple_of(core * HALF, HALF), HALF)
-        swap = remote(g.at[:, theirs], gt, ar_send.at[105], ar_recv.at[105], other_core)
-        swap.start()
+
+        def swap(m):
+            return remote(g.at[m, theirs], gt.at[m], ar_send.at[110 + m], ar_recv.at[110 + m], other_core)
+
+        g[0] = mm_t(dp[...], image)
+        swap(0).start()
+        g[1] = mm_t(res, jnp.where(it == 0, res, image))
+        swap(1).start()
+        g[2] = mm_t(image, image)
+        swap(2).start()
         for i in range(4):
             core_copy(i).wait_send()
         for i in range(3):
             ring_copy(i).wait_send()
-        swap.wait_recv()
-        g0[...] = (g[:, ours] + gt[...]).reshape(3, RING, RING, 8, SIDE)
-        pending = [swap]
+        pending = []
 
         def each(m, fn):
             i, j = here[m], here[(m + 1) % 3]
@@ -339,6 +346,8 @@
             return plane_copy(48, m, k, h0.at[m, i, j], h0.at[m, i, j])
 
         for m in range(3):
+            swap(m).wait_recv()
+            g0[m] = (g[m, ours] + gt[m]).reshape(RING, RING, 8, SIDE)
             each(m, lambda k, i, j: reduce_send(m, k, i, j).start())
             i, j = here[m], here[(m + 1) % 3]
             u1[m, i, j] = g0[m, i, j]
@@ -383,26 +392,25 @@
         first = it == 0
         later = it > 0
         land(0)
-        pl.when(first)(lambda: land(1))
-        joined(0)
 
         @pl.when(first)
         def _():
+            land(1)
             joined(1)
             norm[...] = full[1]
 
         owner_start(0)
         owner_start(1)
+        raw = gf[core, 0, :, :HALF]
+        head = eliminate(jnp.where(core == 0, 0.5 * (raw + raw.T), norm[:HALF, :HALF]), HALF)
+        joined(0)
         raw = full[0]
         mat[...] = jnp.where(core == 0, 0.5 * (raw + raw.T), norm[...])
-        head = eliminate(mat[:HALF, :HALF], HALF)
         t = mm(mat[HALF:, :HALF], head)
         corner = mat[HALF:, HALF:] - mm(t, mat[:HALF, HALF:])
         tri[...] = t
         work[...] = corner
         mat[:HALF, :HALF] = head
-        pl.when(later)(lambda: land(1))
-        land(2)
         tail = eliminate(work[...], HALF)
         t = tri[...]
         low = mm(tail, t)
@@ -412,17 +420,20 @@
         inv[core, HALF:, HALF:] = tail
         share = remote(inv.at[core], inv.at[core], ar_send.at[106], ar_recv.at[106], other_core)
         share.start()
+        pl.when(later)(lambda: land(1))
+        land(2)
+        remote(inv.at[1 - core], inv.at[1 - core], ar_send.at[106], ar_recv.at[106], other_core).wait_recv()
+        alpha = mm(inv[0], norm[...])
         pl.when(later)(lambda: joined(1))
         joined(2)
         cross = jnp.where(first, full[0], full[1])
         for copy in pending:
             copy.wait_send()
         for m in range(3):
+            swap(m).wait_send()
             join(m, core).wait_send()
             each(m, lambda k, i, j: reduce_send(m, k, i, j).wait_send())
             each(m, lambda k, i, j: spread_send(m, k, i, j).wait_send())
-        remote(inv.at[1 - core], inv.at[1 - core], ar_send.at[106], ar_recv.at[106], other_core).wait_recv()
-        alpha = mm(inv[0], norm[...])
         fall = mm(cross, alpha)
         after = norm[...] - fall - fall.T + mm_t(alpha, mm(full[2], alpha))
         beta = mm(inv[1], after)
@@ -472,7 +483,7 @@
             f32(side, side), f32(3, side, side), f32(2, side, side),
             f32(side, side), f32(HALF, HALF), f32(HALF, HALF), f32(2, side, side),
             pltpu.SemaphoreType.DMA,
-            dma(30), dma(30), dma(7), dma(7), dma(3), dma(3), dma(110), dma(110),
+            dma(30), dma(30), dma(7), dma(7), dma(3), dma(3), dma(113), dma(113),
         ],
         compiler_params=pltpu.CompilerParams(
             collective_id=0, has_side_effects=True, vmem_limit_bytes=60 * 1024 * 1024

time: 211 us -> 205 us (0.972)
  Pallas kernels: 210 us -> 205 us
    pallas_call x1, Pallas kernels: 208 us -> 203 us  [body(): pl.pallas_call(kernel, out_shape=(vec, vec, vec), in_specs=[pl.BlockSpec(...]
where the time goes in v6:
time: 205 us
  Pallas kernels  205 us (100%)
    pallas_call x1, Pallas kernels, body(): pl.pallas_call(kernel, out_shape=(vec, vec, vec), in_specs=[pl.BlockSpec(...  203 us

profile of v6, /device:TPU:1, one launch (start us, length us, event | category | flops | bytes accessed | tf_op | source)
XLA Modules:
  0.0 205.3 jit_solution(12877546390024776628)
XLA Ops:
  0.6 202.6 %shard_map.49 = (f32[224,256]{1,0:T(8,128)}, f32[224,256]{1,0:T(8,128)}, f32[224,256]{1,0:T(8,128)}) custom-call(bf16[8,224,3584]{2,1,0:T(8,128)(2,1)} %bitcast.1, f32[224,256]{1,0:T(8,128)} %b_ref.1), custom_call_target="tpu_custom_call" | custom-call | tf_op jit(solution)/shard_map/pallas_call | solution.py:468
  203.3 2.0 shard_map.50

commit v7 on v6

--- a/solution.py
+++ b/solution.py
@@ -441,11 +441,13 @@
         small[0] = alpha
         small[1] = beta
 
-        settle(owner_copy(0))
-        settle(owner_copy(1))
-        r_ref[...] -= mm(q[...], alpha)
         dold[...] = d_ref[...]
-        d_ref[...] = r_ref[...] + mm(d_ref[...], beta)
+        d_ref[...] = mm(d_ref[...], beta)
+        for half in (0, 1):
+            rows = pl.ds(112 * half, 112)
+            settle(owner_copy(half))
+            r_ref[rows] -= mm(q[rows], alpha)
+            d_ref[rows] += r_ref[rows]
         share.wait_send()
         return carry
 

time: 205 us -> 206 us (level)
  no operation moved by 1% of the time
where the time goes in v7:
time: 206 us
  Pallas kernels  205 us (100%)
    pallas_call x1, Pallas kernels, body(): pl.pallas_call(kernel, out_shape=(vec, vec, vec), in_specs=[pl.BlockSpec(...  203 us

profile of v7, /device:TPU:1, one launch (start us, length us, event | category | flops | bytes accessed | tf_op | source)
XLA Modules:
  0.0 206.0 jit_solution(5290691511201925303)
XLA Ops:
  0.6 203.3 %shard_map.49 = (f32[224,256]{1,0:T(8,128)}, f32[224,256]{1,0:T(8,128)}, f32[224,256]{1,0:T(8,128)}) custom-call(bf16[8,224,3584]{2,1,0:T(8,128)(2,1)} %bitcast.1, f32[224,256]{1,0:T(8,128)} %b_ref.1), custom_call_target="tpu_custom_call" | custom-call | tf_op jit(solution)/shard_map/pallas_call | solution.py:470
  203.9 2.0 shard_map.50
